TPU v7x, 128 devices: a whole 4x4x4 slice. The times are simulated.
128 devices in a mesh: section: 8 (over y, core), tp: 16 (over x, z).
Axes of the slice: x: 4, y: 4, z: 4, core: 2. Of those that a mesh axis runs over, the one named last changes fastest.
Arguments:
- stream_in: bfloat16 [512, 8192], P(None, 'tp')
- layer_delta: bfloat16 [8, 512, 8192], P('section', None, 'tp')
- norm_gain: float32 [8192], P('tp'), may hold values from 0.25 to 1.75
- out_embed: bfloat16 [8192, 16384], P(None, 'tp')
- exit_blocks: int32 [8, 4], P('section'), may hold values from 0 to 3
- exit_counts: int32 [8], P('section'), may hold values from 1 to 4, 16 in all
- targets: int32 [512], replicated, may hold values from 0 to 16383
Outputs:
- exit_loss: float32 [8, 4, 128], P('section')
Inputs may be any that keep to these rules, and one draw needn't show every extreme that they name: `exit_counts`: each section scores at least one block, the counts of all sections sum to 2 times the number of sections, and some section scores exactly 4. `exit_blocks`: block numbers of the micro-batch's 128-row blocks; only a section's first exit_counts entries are used.
All inputs are finite; a program needn't handle non-finite values.
Results may differ from a plain program's by a relative error of at most 0.02.
Values may be sent and summed in bfloat16 or wider, within the bound.
A program may use at most 128 MiB of HBM per device.

v0:
```python
import jax
import jax.numpy as jnp
from jax import lax
from jax.sharding import PartitionSpec as P

BLK = 128
MAXB = 4


EPS = 1e-05


def prefix(shard, axis, join, neutral):
    place = lax.axis_index(axis)
    gathered = lax.all_gather(shard.astype(jnp.bfloat16), axis)
    state = jnp.zeros_like(shard) + jnp.asarray(neutral, shard.dtype)

    def one(lap, state):
        return join(state, lax.dynamic_index_in_dim(gathered, lap, 0, False).astype(shard.dtype))

    return lax.fori_loop(0, place, one, state)


def from_root(shard, axis, root):
    mine = lax.axis_index(axis) == root
    return lax.psum(jnp.where(mine, shard, jnp.zeros_like(shard)), axis)


def add_terms(first, second):
    return first + second


def row_losses(exit_rows, teach_rows, target_rows, norm_gain, out_embed):
    width = out_embed.shape[0]
    squares = lax.psum(
        (jnp.sum(exit_rows * exit_rows, axis=1), jnp.sum(teach_rows * teach_rows, axis=1)), "tp"
    )
    normed_exit = (
        exit_rows * lax.rsqrt(squares[0] / width + EPS)[:, None] * norm_gain[None, :]
    ).astype(jnp.bfloat16)
    normed_teach = (
        teach_rows * lax.rsqrt(squares[1] / width + EPS)[:, None] * norm_gain[None, :]
    ).astype(jnp.bfloat16)
    vocab_part = out_embed.shape[1]
    logit_exit = jnp.dot(
        lax.all_gather(normed_exit, "tp", axis=1, tiled=True),
        out_embed,
        preferred_element_type=jnp.float32,
    )
    logit_teach = jnp.dot(
        lax.all_gather(normed_teach, "tp", axis=1, tiled=True),
        out_embed,
        preferred_element_type=jnp.float32,
    )
    first_column = lax.axis_index("tp") * vocab_part
    columns = jnp.arange(vocab_part, dtype=jnp.int32)
    hit = (target_rows - first_column)[:, None] == columns[None, :]
    target_part = jnp.sum(jnp.where(hit, logit_exit, 0.0), axis=1)
    peak_exit, peak_teach = lax.pmax(
        (jnp.max(logit_exit, axis=1), jnp.max(logit_teach, axis=1)), "tp"
    )
    weight_teach = jnp.exp(logit_teach - peak_teach[:, None])
    total_exit, total_teach, cross, picked = lax.psum(
        (
            jnp.sum(jnp.exp(logit_exit - peak_exit[:, None]), axis=1),
            jnp.sum(weight_teach, axis=1),
            jnp.sum(weight_teach * (logit_teach - logit_exit), axis=1),
            target_part,
        ),
        "tp",
    )
    log_exit = jnp.log(total_exit) + peak_exit
    log_teach = jnp.log(total_teach) + peak_teach
    return 2.0 * log_exit - picked + cross / total_teach - log_teach


def body(stream_in, layer_delta, norm_gain, out_embed, exit_blocks, exit_counts, targets):
    stream = stream_in.astype(jnp.float32)
    mine_delta = layer_delta[0].astype(jnp.float32)
    before = prefix(mine_delta, "section", add_terms, jnp.zeros_like(mine_delta))
    exit_all = stream + before + mine_delta
    final_all = from_root(
        exit_all.astype(jnp.bfloat16), "section", lax.axis_size("section") - 1
    ).astype(exit_all.dtype)
    starts = [exit_blocks[0, slot_index] * BLK for slot_index in range(MAXB)]
    exit_rows = jnp.concatenate(
        [lax.dynamic_slice_in_dim(exit_all, start, BLK, 0) for start in starts], axis=0
    )
    teach_rows = jnp.concatenate(
        [lax.dynamic_slice_in_dim(final_all, start, BLK, 0) for start in starts], axis=0
    )
    target_rows = jnp.concatenate(
        [lax.dynamic_slice_in_dim(targets, start, BLK, 0) for start in starts], axis=0
    )
    losses = row_losses(exit_rows, teach_rows, target_rows, norm_gain, out_embed).reshape(MAXB, BLK)
    keep = jnp.arange(MAXB, dtype=jnp.int32) < exit_counts[0]
    return jnp.where(keep[:, None], losses, 0.0)[None]


def solution(mesh):
    placed = (
        P(None, "tp"),
        P("section", None, "tp"),
        P("tp"),
        P(None, "tp"),
        P("section", None),
        P("section"),
        P(),
    )
    return jax.shard_map(
        body, mesh=mesh, in_specs=placed, out_specs=P("section", None, None), check_vma=False
    )
```

profile of v0, /device:TPU:0, one launch (start us, length us, event | category | flops | bytes accessed | tf_op | source)
XLA Modules:
  0.0 407.7 jit_solution(8671719075948042999)
XLA Ops:
  6.5 0.0 all-gather.4.cloned.1.call-start
  6.5 0.7 all-gather.4.cloned.1.call-update
  7.3 0.0 all-reduce.5.cloned.1.call-start
  7.3 36.3 %all-gather.4.cloned.1.call-done = bf16[8,512,512]{2,1,0:T(8,128)(2,1)} async-done(((bf16[1,512,512]{2,1,0:T(8,128)(2,1)}), bf16[8,512,512]{2,1,0:T(8,128)(2,1)}) %all-gather.4.cloned.1.call-update) | async-done | bytes 4194320 | tf_op jit(solution)/shard_map/all_gather | solution.py:15
  43.6 0.1 broadcast_in_dim.21
  43.8 0.0 copy-start
  43.8 0.0 copy-start.1
  43.8 1.0 copy-done
  44.8 0.3 copy-done.1
  45.1 0.0 copy-start.2
  45.1 1.1 convert_select_fusion
  46.2 0.0 all-reduce.5.cloned.1.call-update
  46.2 0.0 all-gather.8.cloned.1.call-start
  46.2 0.0 copy-done.2
  46.2 0.7 fusion.3
  49.5 0.1 constant_dynamic-slice_fusion.7
  49.6 0.1 multiply_reduce_fusion.2
  49.8 0.0 copy-start.4
  49.8 64.8 %all-reduce.5.cloned.1.call-done = bf16[512,512]{1,0:T(8,128)(2,1)} async-done(((bf16[512,512]{1,0:T(8,128)(2,1)}), bf16[512,512]{1,0:T(8,128)(2,1)}) %all-reduce.5.cloned.1.call-update) | async-done | bytes 524304 | tf_op jit(solution)/shard_map/psum | solution.py:26
  114.6 1.2 convert_element_type.33
  115.8 0.1 constant_dynamic-slice_fusion.3
  115.9 0.2 multiply_reduce_fusion.1
  116.0 40.5 %all-reduce.1 = (f32[512]{0:T(512)S(1)}, f32[512]{0:T(512)S(1)}) all-reduce(f32[512]{0:T(512)S(1)} %multiply_reduce_fusion.1, f32[512]{0:T(512)S(1)} %multiply_reduce_fusion.2), channel_id=1, replica_groups=mesh['section'=8,'tp'=16] {'tp'}, use_global_device_ids=true, to_apply=%region_12.13 | all-reduce | flops 1024 | bytes 8192 | tf_op jit(solution)/shard_map/psum | solution.py:35
  156.6 0.0 copy-done.4
  156.6 0.0 copy-start.3
  156.6 1.3 multiply_convert_fusion.1
  157.8 0.0 all-gather.8.cloned.1.call-update
  157.9 0.0 all-gather.6.cloned.1.call-start
  157.9 0.5 all-gather.6.cloned.1.call-update
  159.1 0.0 copy-done.3
  159.1 0.1 fusion.2
  159.2 69.9 %all-gather.8.cloned.1.call-done = bf16[512,8192]{1,0:T(8,128)(2,1)} async-done(((bf16[512,512]{1,0:T(8,128)(2,1)}), bf16[512,8192]{1,0:T(8,128)(2,1)}) %all-gather.8.cloned.1.call-update) | async-done | bytes 8388624 | tf_op jit(solution)/shard_map/all_gather | solution.py:51
  229.1 14.8 %fusion.4 = (f32[512]{0:T(512)S(1)}, f32[512,1024]{1,0:T(8,128)S(1)}) fusion(bf16[512,8192]{1,0:T(8,128)(2,1)} %all-gather.8.cloned.1.call-done, bf16[8192,1024]{1,0:T(8,128)(2,1)} %param.12), kind=kOutput, calls=%fused_computation.31 | convolution fusion | flops 8590458880 | bytes 27265024 | tf_op jit(solution)/shard_map/dot_general | solution.py:50
  243.9 63.8 %all-gather.6.cloned.1.call-done = bf16[512,8192]{1,0:T(8,128)(2,1)} async-done(((bf16[512,512]{1,0:T(8,128)(2,1)}), bf16[512,8192]{1,0:T(8,128)(2,1)}) %all-gather.6.cloned.1.call-update) | async-done | bytes 8388624 | tf_op jit(solution)/shard_map/all_gather | solution.py:46
  307.7 16.0 %fusion.1 = (f32[512]{0:T(512)S(1)}, f32[512]{0:T(512)S(1)}, f32[512,1024]{1,0:T(8,128)}) fusion(s32[512]{0:T(512)S(1)} %add_subtract_fusion, bf16[512,8192]{1,0:T(8,128)(2,1)} %all-gather.6.cloned.1.call-done, bf16[8192,1024]{1,0:T(8,128)(2,1)} %param.12), kind=kOutput, calls=%fused_computation.28 | convolution fusion | flops 8592031744 | bytes 27269120 | tf_op jit(solution)/shard_map/dot_general | solution.py:45
  323.7 38.1 %all-reduce.2 = (f32[512]{0:T(512)S(1)}, f32[512]{0:T(512)S(1)}) all-reduce(f32[512]{0:T(512)S(1)} %get-tuple-element.70, f32[512]{0:T(512)S(1)} %get-tuple-element.32), channel_id=1, replica_groups=mesh['section'=8,'tp'=16] {'tp'}, use_global_device_ids=true, to_apply=%region_14.15 | all-reduce | flops 1024 | bytes 8192 | tf_op jit(solution)/shard_map/pmax | solution.py:59
  361.8 2.7 multiply_reduce_fusion
  364.5 35.9 %all-reduce = (f32[512]{0:T(512)S(1)}, f32[512]{0:T(512)S(1)}, f32[512]{0:T(512)S(1)}, f32[512]{0:T(512)S(1)}) all-reduce(f32[512]{0:T(512)S(1)} %get-tuple-element.30, f32[512]{0:T(512)S(1)} %get-tuple-element.29, f32[512]{0:T(512)S(1)} %get-tuple-element.33, f32[512]{0:T(512)S(1)} %get-tuple-element.31), channel_id=1, replica_groups=mesh['section'=8,'tp'=16] {'tp'}, use_global_device_ids=true, to_apply=%region_18.19 | all-reduce | flops 2048 | bytes 16384 | tf_op jit(solution)/shard_map/psum | solution.py:63
  400.5 0.7 bitcast_select_fusion
  (4 shorter events, 0.0 us)
Async XLA Ops:
  6.5 37.1 %all-gather.4.cloned.1.call-start = ((), (), s32[]{:S(2)}) async-start(), calls=%async_computation | async-start | bytes 4718592 | tf_op jit(solution)/shard_map/all_gather | solution.py:15
  7.3 107.4 %all-reduce.5.cloned.1.call-start = ((), (), s32[]{:S(2)}) async-start(), calls=%async_computation.2 | async-start | bytes 1048576 | tf_op jit(solution)/shard_map/psum | solution.py:26
  43.8 1.0 copy-start
  43.8 1.3 copy-start.1
  45.1 1.1 copy-start.2
  46.2 182.9 %all-gather.8.cloned.1.call-start = ((), (), s32[]{:S(2)}) async-start(), calls=%async_computation.3 | async-start | bytes 8912896 | tf_op jit(solution)/shard_map/all_gather | solution.py:51
  49.8 106.8 %copy-start.4 = (f32[512]{0:T(512)S(1)}, f32[512]{0:T(512)}, u32[]{:S(2)}) copy-start(f32[512]{0:T(512)} %param.11) | copy-start | bytes 6148
  156.6 2.5 copy-start.3
  157.9 149.8 %all-gather.6.cloned.1.call-start = ((), (), s32[]{:S(2)}) async-start(), calls=%async_computation.1 | async-start | bytes 8912896 | tf_op jit(solution)/shard_map/all_gather | solution.py:46
Sparse Core Ops, SparseCore 0:
  9.0 34.5 all-gather.3
  46.3 68.2 all-reduce.4
  158.0 71.0 all-gather.7
  231.1 76.6 all-gather.5
where the time goes:
time: 408 us
  waiting for transfers between devices  236 us (58%)
  blocking collectives  115 us (28%)
  matrix products  30.8 us (8%)
  between operations  16.5 us (4%)
  other arithmetic  7.16 us (2%)
    all_gather x1, waiting for transfers between devices, row_losses(): lax.all_gather(normed_teach, 'tp', axis=1, tiled=True)  69.9 us
    psum x1, waiting for transfers between devices, from_root(): return lax.psum(jnp.where(mine, shard, jnp.zeros_like(shard)), axis)  64.8 us
    all_gather x1, waiting for transfers between devices, row_losses(): lax.all_gather(normed_exit, 'tp', axis=1, tiled=True)  63.8 us
    psum x1, blocking collectives, row_losses(): lax.psum((jnp.sum(exit_rows * exit_rows, axis=1), jnp.sum(teach_rows * te...  40.5 us
    pmax x1, blocking collectives, row_losses(): lax.pmax((jnp.max(logit_exit, axis=1), jnp.max(logit_teach, axis=1)), 'tp')  38.1 us
    all_gather x1, waiting for transfers between devices, prefix(): gathered = lax.all_gather(shard.astype(jnp.bfloat16), axis)  36.3 us
    psum x1, blocking collectives, row_losses(): lax.psum((jnp.sum(jnp.exp(logit_exit - peak_exit[:, None]), axis=1), jnp....  35.9 us
    dot_general x1, matrix products, row_losses(): jnp.dot(lax.all_gather(normed_exit, 'tp', axis=1, tiled=True), out_embed,...  16 us
  transfers between devices with their start and end apart: 4, of which 4 were waited for; matrix products, arithmetic and copies ran while one was open for 4% of the time, Pallas kernels for 0%

commit v1 on v0

v1 whole, which is shorter than its diff:
```python
import functools
import itertools

import jax
import jax.numpy as jnp
from jax import lax
from jax.experimental import pallas as pl
from jax.experimental.pallas import tpu as pltpu
from jax.sharding import PartitionSpec as P

BLK = 128
MAXB = 4
EPS = 1e-05
NS = 8
TX = 4
TZ = 4
NT = TX * TZ
SUB = BLK // NS
NPAIR = 2 * NS
NB = 4
NG = NPAIR - 1 + NB
ROWS = NG * SUB
LANE = 128
NC = 4
WIDTH = LANE * NC * NT
VPART = 1024
NTILE = 512
DOWN = 2.0 ** -58
UP = 2.0 ** 58
F32 = jnp.float32
MESH = pl.DeviceIdType.MESH
ORDER = (0, 2, 1, 3)


def long_sign(c):
    return 1 if c % 2 == 0 else -1


def rel_of(c, a, b):
    dx, dz = (a, b) if c < NC // 2 else (b, a)
    return (dx % TX) * TZ + dz % TZ


def step_of(c, axis, sign):
    along_x = (axis == 0) == (c < NC // 2)
    return (sign, 0) if along_x else (0, sign)


def forwards(c, a, b):
    go = long_sign(c)
    if (a, b) == (0, 0):
        return [(0, go), (0, -go), (1, go), (1, -go)]
    if b == 0:
        out = [(0, go)] if a == -go else []
        return out + [(1, go), (1, -go)]
    return [(1, go)] if b == -go else []


def wrap(v):
    v = v % 4
    return v - 4 if v == 3 else v


def events():
    out = []
    for dist in range(1, 5):
        for c in ORDER:
            go = long_sign(c)
            places = [(2, 0), (-go, 0), (go, 0), (2, -go), (2, go), (-go, -go), (go, -go), (0, -go)]
            places += [(-go, go), (go, go), (0, go), (0, 2), (-go, 2), (go, 2), (2, 2)]
            out += [(c, a, b) for a, b in places if abs(a) + abs(b) == dist]
    return out


def plan():
    ready = {(0, 0): 2, (0, 1): 2}
    queue = [(0, 0), (0, 1)]
    steps = []
    for c, a, b in events():
        steps.append(("wait", c, a, b))
        key = (rel_of(c, a, b), c // 2)
        ready[key] = ready.get(key, 0) + 1
        if ready[key] == 2:
            queue.append(key)
        if queue:
            steps.append(("dot",) + queue.pop(0))
    return steps + [("dot",) + key for key in queue]


STEPS = plan()
FIRST_USE = list(dict.fromkeys(s[1] for s in STEPS if s[0] == "dot"))


def merge(parts):
    peak_e = functools.reduce(jnp.maximum, [p[0:1] for p in parts])
    peak_t = functools.reduce(jnp.maximum, [p[2:3] for p in parts])
    sum_e = sum_t = cross = picked = 0.0
    for p in parts:
        fe = jnp.exp(p[0:1] - peak_e)
        ft = jnp.exp(p[2:3] - peak_t)
        sum_e = sum_e + p[1:2] * fe
        sum_t = sum_t + p[3:4] * ft
        cross = cross + p[4:5] * ft
        picked = picked + p[5:6]
    return peak_e, sum_e, peak_t, sum_t, cross, picked


def kernel(
    eb_hbm, ec_hbm, gain_hbm, tgt_hbm, stream_hbm, delta_hbm, w_hbm, out_ref,
    eb_s, ec_s, meta_s, own_s, blk_s, grp_s,
    gain_v, tgt_v, stream_v, meta_src, meta_v, abuf, hid, sq, gath, wv, acc,
    ss_x, ss_z, scale_v, prob_v, tstat, tcol, pst, st_x, st_z, loss_y, tot_v,
    loc_sem, w_sem, meta_send, meta_recv, a_send, a_recv, g_send, g_recv, ex_send, ex_recv, y_send, y_recv,
):
    sec = lax.axis_index("section")
    tp = lax.axis_index("tp")
    px, pz = tp // TZ, tp % TZ

    def plane(dx, dz):
        return (sec, ((px + dx) % TX) * TZ + (pz + dz) % TZ)

    sec_peers = [((sec + k) % NS, tp) for k in range(1, NS)]
    x_peers = [plane(k, 0) for k in range(1, TX)]
    z_peers = [plane(0, k) for k in range(1, TZ)]
    everyone = sec_peers + x_peers + z_peers

    barrier = pltpu.get_barrier_semaphore()
    for peer in everyone:
        pl.semaphore_signal(barrier, inc=1, device_id=peer, device_id_type=MESH)

    local = [
        pltpu.make_async_copy(eb_hbm, eb_s, loc_sem.at[0]),
        pltpu.make_async_copy(ec_hbm, ec_s, loc_sem.at[1]),
        pltpu.make_async_copy(stream_hbm.at[:, sec], stream_v, loc_sem.at[2]),
        pltpu.make_async_copy(gain_hbm, gain_v, loc_sem.at[3]),
        pltpu.make_async_copy(tgt_hbm, tgt_v, loc_sem.at[4]),
    ]
    own_delta = [
        pltpu.make_async_copy(
            delta_hbm.at[:, sec, :, pl.ds(c * LANE, LANE)], abuf.at[c, sec], loc_sem.at[5 + c]
        )
        for c in range(NC)
    ]
    for copy in local + own_delta:
        copy.start()

    local[0].wait()
    local[1].wait()
    lane1 = lax.broadcasted_iota(jnp.int32, (1, LANE), 1)
    info = jnp.where(lane1 == MAXB, ec_s[0], 0)
    for k in range(MAXB):
        info = jnp.where(lane1 == k, eb_s[0, k], info)
    meta_src[...] = info
    meta_v[pl.ds(sec, 1), :, :] = info[None]

    pl.semaphore_wait(barrier, len(everyone))

    sends = []

    def send(src, dst, send_sem, recv_sem, peer):
        copy = pltpu.make_async_remote_copy(
            src_ref=src, dst_ref=dst, send_sem=send_sem, recv_sem=recv_sem,
            device_id=peer, device_id_type=MESH,
        )
        copy.start()
        sends.append(copy)

    def arrived(dst, recv_sem, any_sem):
        pltpu.make_async_remote_copy(
            src_ref=dst, dst_ref=dst, send_sem=any_sem, recv_sem=recv_sem,
            device_id=x_peers[0], device_id_type=MESH,
        ).wait_recv()

    for k, peer in enumerate(sec_peers):
        send(meta_src, meta_v.at[sec], meta_send.at[k], meta_recv.at[sec], peer)
    for c in ORDER:
        for k, peer in enumerate(sec_peers):
            send(
                delta_hbm.at[:, peer[0], :, pl.ds(c * LANE, LANE)], abuf.at[c, sec],
                a_send.at[c, k], a_recv.at[c, sec], peer,
            )

    w_copies = {}
    for i, rel in enumerate(FIRST_USE):
        src_tp = ((px + rel // TZ) % TX) * TZ + (pz + rel % TZ) % TZ
        w_copies[rel] = pltpu.make_async_copy(w_hbm.at[src_tp], wv.at[rel], w_sem.at[i])
        w_copies[rel].start()

    for peer in sec_peers:
        arrived(meta_v.at[peer[0]], meta_recv.at[peer[0]], meta_send.at[0])
    to_smem = pltpu.make_async_copy(meta_v, meta_s, loc_sem.at[9])
    to_smem.start()
    to_smem.wait()
    counts = [meta_s[u, 0, MAXB] for u in range(NS)]
    offs = [jnp.int32(0)]
    for u in range(NS - 1):
        offs.append(offs[-1] + counts[u])
    for j in range(NPAIR):
        owner = jnp.int32(0)
        base = jnp.int32(0)
        for u in range(1, NS):
            owner = jnp.where(offs[u] <= j, u, owner)
            base = jnp.where(offs[u] <= j, offs[u], base)
        block = meta_s[owner, 0, j - base]
        own_s[j] = owner
        blk_s[j] = block
        grp_s[j] = j if j < NPAIR - 1 else NPAIR - 1 + block

    local[2].wait()
    local[3].wait()
    local[4].wait()
    lane_r = lax.broadcasted_iota(jnp.int32, (SUB, LANE), 1)
    sub_r = lax.broadcasted_iota(jnp.int32, (SUB, LANE), 0)
    mine = lane_r == sec * SUB + sub_r
    for b in range(NB):
        row = jnp.broadcast_to(tgt_v[b : b + 1, :].astype(F32), (SUB, LANE))
        col = jnp.sum(jnp.where(mine, row, 0.0), axis=1, keepdims=True)
        tcol[b] = jnp.broadcast_to(col, (SUB, LANE)) - (tp * VPART).astype(F32)

    hop = itertools.count()

    def pass_on(c, a, b):
        rel = rel_of(c, a, b)
        for axis, sign in forwards(c, a, b):
            aa, bb = (wrap(a - sign), b) if axis == 0 else (a, wrap(b - sign))
            there = rel_of(c, aa, bb)
            send(
                gath.at[rel, c], gath.at[there, c],
                g_send.at[next(hop)], g_recv.at[there, c],
                plane(*step_of(c, axis, sign)),
            )

    for n, c in enumerate(ORDER):
        own_delta[c].wait()
        for peer in sec_peers:
            arrived(abuf.at[c, peer[0]], a_recv.at[c, peer[0]], a_send.at[0, 0])
        lanes = pl.ds(c * LANE, LANE)
        state = stream_v[:, :, lanes].astype(F32)
        for u in range(NS):
            state = state + abuf[c, u].astype(F32)
            hid[u] = state
        gain = gain_v[c : c + 1, :] * DOWN

        def put(g, rows, c=c, n=n, gain=gain):
            sq[g] = rows * rows if n == 0 else sq[g] + rows * rows
            gath[0, c, pl.ds(g * SUB, SUB), :] = (rows * gain).astype(jnp.bfloat16)

        for j in range(NPAIR - 1):
            put(j, hid[own_s[j], blk_s[j]])
        for b in range(NB):
            put(NPAIR - 1 + b, hid[NS - 1, b])
        pass_on(c, 0, 0)

    for g in range(NG, 24):
        sq[g] = jnp.zeros((SUB, LANE), F32)
    sums = []
    for q in range(3):
        part = sq[pl.ds(q * 8, 8)].reshape(LANE, LANE)
        sums.append(jnp.sum(part.T, axis=0, keepdims=True))
    ss_x[px] = jnp.concatenate(sums + [jnp.zeros((5, LANE), F32)], axis=0)

    def share(buf, place, peers, stage):
        for k, peer in enumerate(peers):
            send(buf.at[place], buf.at[place], ex_send.at[stage, k], ex_recv.at[stage, place], peer)

    def collect(buf, place, stage):
        for k in range(1, 4):
            there = (place + k) % 4
            arrived(buf.at[there], ex_recv.at[stage, there], ex_send.at[stage, 0])

    share(ss_x, px, x_peers, 0)

    seen = set()
    waits = 0
    for step in STEPS:
        if step[0] == "wait":
            _, c, a, b = step
            rel = rel_of(c, a, b)
            arrived(gath.at[rel, c], g_recv.at[rel, c], g_send.at[0])
            pass_on(c, a, b)
            waits += 1
            if waits == 12:
                collect(ss_x, px, 0)
                ss_z[pz] = ss_x[0] + ss_x[1] + ss_x[2] + ss_x[3]
                share(ss_z, pz, z_peers, 1)
            if waits == 36:
                collect(ss_z, pz, 1)
                total = ss_z[0] + ss_z[1] + ss_z[2] + ss_z[3]
                scale = lax.rsqrt(total / WIDTH + EPS) * UP
                for q in range(3):
                    wide = jnp.broadcast_to(scale[q : q + 1, :], (LANE, LANE)).T
                    scale_v[pl.ds(q * 8, 8)] = wide.reshape(8, SUB, LANE)
        else:
            _, rel, half = step
            if rel not in seen:
                w_copies[rel].wait()
            first = not seen
            seen.add(rel)

            def tile(n, carry, rel=rel, half=half, first=first):
                cols = pl.ds(pl.multiple_of(n * NTILE, NTILE), NTILE)
                lhs = jnp.concatenate([gath[rel, 2 * half], gath[rel, 2 * half + 1]], axis=1)
                rhs = wv[rel, pl.ds(half * 2 * LANE, 2 * LANE), cols]
                part = jnp.dot(lhs, rhs, preferred_element_type=F32).reshape(NG, SUB, NTILE)
                acc[:, :, cols] = part if first else acc[:, :, cols] + part
                return carry

            lax.fori_loop(0, VPART // NTILE, tile, 0)

    def wide8(v):
        return jnp.concatenate([v] * (VPART // LANE), axis=1)

    def teach(b, carry):
        logit = acc[NPAIR - 1 + b] * wide8(scale_v[NPAIR - 1 + b])
        peak = jnp.max(logit, axis=1, keepdims=True)
        weight = jnp.exp(logit - peak)
        prob_v[b] = weight
        total = jnp.sum(weight, axis=1, keepdims=True)
        tstat[b] = jnp.where(lane_r == 2, peak, jnp.where(lane_r == 3, total, 0.0))
        return carry

    lax.fori_loop(0, NB, teach, 0)
    column = lax.broadcasted_iota(jnp.int32, (SUB, VPART), 1).astype(F32)

    def leave(j, carry):
        block = blk_s[j]
        group = grp_s[j]
        exit_logit = acc[group] * wide8(scale_v[group])
        teach_logit = acc[NPAIR - 1 + block] * wide8(scale_v[NPAIR - 1 + block])
        weight = prob_v[block]
        peak = jnp.max(exit_logit, axis=1, keepdims=True)
        total = jnp.sum(jnp.exp(exit_logit - peak), axis=1, keepdims=True)
        cross = jnp.sum(weight * (teach_logit - exit_logit), axis=1, keepdims=True)
        hit = wide8(tcol[block]) == column
        picked = jnp.sum(jnp.where(hit, exit_logit, 0.0), axis=1, keepdims=True)
        out = tstat[block]
        for k, v in ((0, peak), (1, total), (4, cross), (5, picked)):
            out = jnp.where(lane_r == k, v, out)
        pst[j] = out
        return carry

    lax.fori_loop(0, NPAIR, leave, 0)
    stats = [pst[pl.ds(q * 8, 8)].reshape(LANE, LANE).T[0:8, :] for q in range(2)]
    st_x[px] = jnp.concatenate(stats, axis=1)
    share(st_x, px, x_peers, 2)
    collect(st_x, px, 2)
    joined = merge([st_x[i] for i in range(TX)])
    st_z[pz] = jnp.concatenate(list(joined) + [jnp.zeros((2, NPAIR * SUB), F32)], axis=0)
    share(st_z, pz, z_peers, 3)
    collect(st_z, pz, 3)
    peak_e, sum_e, peak_t, sum_t, cross, picked = merge([st_z[i] for i in range(TZ)])
    log_e = jnp.log(sum_e) + peak_e
    log_t = jnp.log(sum_t) + peak_t
    loss = 2.0 * log_e - picked + cross / sum_t - log_t

    at = lax.broadcasted_iota(jnp.int32, (NPAIR, NPAIR * SUB), 1) // SUB
    pair = lax.broadcasted_iota(jnp.int32, (NPAIR, NPAIR * SUB), 0)
    spread = jnp.where(at == pair, jnp.broadcast_to(loss, (NPAIR, NPAIR * SUB)), 0.0)
    spread = spread[:, :LANE] + spread[:, LANE:]
    for shift in (64, 32, 16):
        spread = spread + pltpu.roll(spread, shift, 1)
    place = lax.broadcasted_iota(jnp.int32, (NPAIR, LANE), 1) // SUB
    loss_y[sec] = jnp.where(place == sec, spread, 0.0)
    for k, peer in enumerate(sec_peers):
        send(loss_y.at[sec], loss_y.at[sec], y_send.at[k], y_recv.at[sec], peer)
    for peer in sec_peers:
        arrived(loss_y.at[peer[0]], y_recv.at[peer[0]], y_send.at[0])
    total = loss_y[0]
    for u in range(1, NS):
        total = total + loss_y[u]
    tot_v[pl.ds(0, NPAIR)] = total
    tot_v[pl.ds(NPAIR, 8)] = jnp.zeros((8, LANE), F32)
    start = jnp.int32(0)
    for u in range(NS):
        start = start + jnp.where(u < sec, counts[u], 0)
    for k in range(MAXB):
        row = tot_v[pl.ds(start + k, 1), :]
        out_ref[0, pl.ds(k, 1), :] = jnp.where(k < ec_s[0], row, 0.0)
    for copy in sends:
        copy.wait_send()


def body(stream_in, layer_delta, norm_gain, out_embed, exit_blocks, exit_counts, targets):
    feat = stream_in.shape[1]
    any_spec = pl.BlockSpec(memory_space=pl.ANY)
    dma = pltpu.SemaphoreType.DMA
    bf16, i32 = jnp.bfloat16, jnp.int32
    vm = pltpu.VMEM
    return pl.pallas_call(
        kernel,
        out_shape=jax.ShapeDtypeStruct((1, MAXB, BLK), F32),
        in_specs=[any_spec] * 7,
        out_specs=pl.BlockSpec(memory_space=pltpu.VMEM),
        scratch_shapes=[
            pltpu.SMEM((1, MAXB), i32),
            pltpu.SMEM((1,), i32),
            pltpu.SMEM((NS, 1, LANE), i32),
            pltpu.SMEM((NPAIR,), i32),
            pltpu.SMEM((NPAIR,), i32),
            pltpu.SMEM((NPAIR,), i32),
            vm((NC, LANE), F32),
            vm((NB, BLK), i32),
            vm((NB, SUB, feat), bf16),
            vm((1, LANE), i32),
            vm((NS, 1, LANE), i32),
            vm((NC, NS, NB, SUB, LANE), bf16),
            vm((NS, NB, SUB, LANE), F32),
            vm((24, SUB, LANE), F32),
            vm((NT, NC, ROWS, LANE), bf16),
            vm((NT, NC * LANE, VPART), bf16),
            vm((NG, SUB, VPART), F32),
            vm((TX, 8, LANE), F32),
            vm((TZ, 8, LANE), F32),
            vm((24, SUB, LANE), F32),
            vm((NB, SUB, VPART), F32),
            vm((NB, SUB, LANE), F32),
            vm((NB, SUB, LANE), F32),
            vm((NPAIR, SUB, LANE), F32),
            vm((TX, 8, NPAIR * SUB), F32),
            vm((TZ, 8, NPAIR * SUB), F32),
            vm((NS, NPAIR, LANE), F32),
            vm((24, LANE), F32),
            dma((10,)),
            dma((NT,)),
            dma((NS - 1,)),
            dma((NS,)),
            dma((NC, NS - 1)),
            dma((NC, NS)),
            dma((NC * (NT - 1),)),
            dma((NT, NC)),
            dma((4, 3)),
            dma((4, 4)),
            dma((NS - 1,)),
            dma((NS,)),
        ],
        compiler_params=pltpu.CompilerParams(
            collective_id=0, has_side_effects=True, vmem_limit_bytes=48 * 1024 * 1024
        ),
    )(
        exit_blocks,
        exit_counts,
        norm_gain.reshape(NC, LANE),
        targets.reshape(NB, BLK),
        stream_in.reshape(NB, NS, SUB, feat),
        layer_delta.reshape(NB, NS, SUB, feat),
        out_embed.reshape(NT, NC * LANE, VPART),
    )


def solution(mesh):
    placed = (
        P(None, "tp"),
        P("section", None, "tp"),
        P("tp"),
        P(None, "tp"),
        P("section", None),
        P("section"),
        P(),
    )
    return jax.shard_map(
        body, mesh=mesh, in_specs=placed, out_specs=P("section", None, None), check_vma=False
    )
```

time: 408 us -> 66.2 us (0.16)
  the two profiles are of different devices: /device:TPU:0 before, /device:TPU:1 now
where the time goes in v1:
time: 66.2 us; the launch traced here: 65.9 us
  Pallas kernels  60.6 us (92%)
  local copies, waits for them, and re-layouts  4.67 us (7%)
  between operations  0.67 us (1%)
    pallas_call x1, Pallas kernels, body(): pl.pallas_call(kernel, out_shape=jax.ShapeDtypeStruct((1, MAXB, BLK), F32...  60.6 us
    unnamed x11, local copies, waits for them, and re-layouts  4.67 us

profile of v1, /device:TPU:1, one launch (start us, length us, event | category | flops | bytes accessed | tf_op | source)
XLA Modules:
  0.0 65.9 jit_solution(17191841505997239038)
XLA Ops:
  0.7 0.0 copy-start
  0.7 1.0 %copy-done = bf16[512,512]{1,0:T(8,128)(2,1)S(1)} copy-done((bf16[512,512]{1,0:T(8,128)(2,1)S(1)}, bf16[512,512]{1,0:T(8,128)(2,1)}, u32[]{:S(2)}) %copy-start) | copy-done | bytes 524312
  1.7 0.0 copy-start.1
  1.7 1.0 %copy-done.1 = bf16[1,512,512]{2,1,0:T(8,128)(2,1)S(1)} copy-done((bf16[1,512,512]{2,1,0:T(8,128)(2,1)S(1)}, bf16[1,512,512]{2,1,0:T(8,128)(2,1)}, u32[]{:S(2)}) %copy-start.1) | copy-done | bytes 524312
  2.7 0.0 copy-start.2
  2.7 0.7 %copy-done.2 = f32[512]{0:T(512)S(1)} copy-done((f32[512]{0:T(512)S(1)}, f32[512]{0:T(512)}, u32[]{:S(2)}) %copy-start.2) | copy-done | bytes 2072
  3.4 0.0 copy-start.3
  3.4 0.7 %copy-done.3 = s32[512]{0:T(512)S(1)} copy-done((s32[512]{0:T(512)S(1)}, s32[512]{0:T(512)}, u32[]{:S(2)}) %copy-start.3) | copy-done | bytes 2072
  4.1 0.0 copy-start.4
  4.1 0.7 copy-done.4
  4.8 60.6 %shard_map.73 = f32[1,4,128]{2,1,0:T(4,128)S(1)} custom-call(s32[1,4]{1,0:T(1,128)S(1)} %copy-done.4, s32[1]{0:T(128)S(6)} %copy.9.ec_hbm, f32[4,128]{1,0:T(4,128)S(1)} %bitcast.7, s32[4,128]{1,0:T(4,128)S(1)} %bitcast.8, bf16[4,8,16,512]{3,2,1,0:T(8,128)(2,1)S(1)} %bitcast.5, bf16[4,8,16,512]{3,2,1,0:T(8,128)(2,1)S(1)} %bitcast.6, ...), custom_call_target="tpu_custom_call" | custom-call | tf_op jit(solution)/shard_map/pallas_call | solution.py:389
  65.4 0.6 copy.10
Async XLA Ops:
  0.7 1.0 %copy-start = (bf16[512,512]{1,0:T(8,128)(2,1)S(1)}, bf16[512,512]{1,0:T(8,128)(2,1)}, u32[]{:S(2)}) copy-start(bf16[512,512]{1,0:T(8,128)(2,1)} %param.7) | copy-start | bytes 1572868
  1.7 1.0 %copy-start.1 = (bf16[1,512,512]{2,1,0:T(8,128)(2,1)S(1)}, bf16[1,512,512]{2,1,0:T(8,128)(2,1)}, u32[]{:S(2)}) copy-start(bf16[1,512,512]{2,1,0:T(8,128)(2,1)} %param.8) | copy-start | bytes 1572868
  2.7 0.7 %copy-start.2 = (f32[512]{0:T(512)S(1)}, f32[512]{0:T(512)}, u32[]{:S(2)}) copy-start(f32[512]{0:T(512)} %param.9) | copy-start | bytes 6148
  3.4 0.7 %copy-start.3 = (s32[512]{0:T(512)S(1)}, s32[512]{0:T(512)}, u32[]{:S(2)}) copy-start(s32[512]{0:T(512)} %param.13) | copy-start | bytes 6148
  4.1 0.7 copy-start.4

commit v2 on v1

--- a/solution.py
+++ b/solution.py
@@ -24,7 +24,7 @@
 NC = 4
 WIDTH = LANE * NC * NT
 VPART = 1024
-NTILE = 512
+NTILE = 1024
 DOWN = 2.0 ** -58
 UP = 2.0 ** 58
 F32 = jnp.float32
@@ -108,7 +108,7 @@
 def kernel(
     eb_hbm, ec_hbm, gain_hbm, tgt_hbm, stream_hbm, delta_hbm, w_hbm, out_ref,
     eb_s, ec_s, meta_s, own_s, blk_s, grp_s,
-    gain_v, tgt_v, stream_v, meta_src, meta_v, abuf, hid, sq, gath, wv, acc,
+    gain_v, tgt_v, stream_v, delta_v, abuf, hid, sq, gath, wv, acc,
     ss_x, ss_z, scale_v, prob_v, tstat, tcol, pst, st_x, st_z, loss_y, tot_v,
     loc_sem, w_sem, meta_send, meta_recv, a_send, a_recv, g_send, g_recv, ex_send, ex_recv, y_send, y_recv,
 ):
@@ -141,18 +141,17 @@
         )
         for c in range(NC)
     ]
-    for copy in local + own_delta:
+    all_delta = pltpu.make_async_copy(delta_hbm, delta_v, loc_sem.at[10])
+    for copy in local[:2] + [all_delta] + local[2:] + own_delta:
         copy.start()
 
     local[0].wait()
     local[1].wait()
-    lane1 = lax.broadcasted_iota(jnp.int32, (1, LANE), 1)
-    info = jnp.where(lane1 == MAXB, ec_s[0], 0)
     for k in range(MAXB):
-        info = jnp.where(lane1 == k, eb_s[0, k], info)
-    meta_src[...] = info
-    meta_v[pl.ds(sec, 1), :, :] = info[None]
-
+        meta_s[sec, 0, k] = eb_s[0, k]
+    meta_s[sec, 0, MAXB] = ec_s[0, 0]
+
+    all_delta.wait()
     pl.semaphore_wait(barrier, len(everyone))
 
     sends = []
@@ -172,11 +171,11 @@
         ).wait_recv()
 
     for k, peer in enumerate(sec_peers):
-        send(meta_src, meta_v.at[sec], meta_send.at[k], meta_recv.at[sec], peer)
+        send(meta_s.at[sec], meta_s.at[sec], meta_send.at[k], meta_recv.at[sec], peer)
     for c in ORDER:
         for k, peer in enumerate(sec_peers):
             send(
-                delta_hbm.at[:, peer[0], :, pl.ds(c * LANE, LANE)], abuf.at[c, sec],
+                delta_v.at[:, peer[0], :, pl.ds(c * LANE, LANE)], abuf.at[c, sec],
                 a_send.at[c, k], a_recv.at[c, sec], peer,
             )
 
@@ -187,10 +186,7 @@
         w_copies[rel].start()
 
     for peer in sec_peers:
-        arrived(meta_v.at[peer[0]], meta_recv.at[peer[0]], meta_send.at[0])
-    to_smem = pltpu.make_async_copy(meta_v, meta_s, loc_sem.at[9])
-    to_smem.start()
-    to_smem.wait()
+        arrived(meta_s.at[peer[0]], meta_recv.at[peer[0]], meta_send.at[0])
     counts = [meta_s[u, 0, MAXB] for u in range(NS)]
     offs = [jnp.int32(0)]
     for u in range(NS - 1):
@@ -201,7 +197,7 @@
         for u in range(1, NS):
             owner = jnp.where(offs[u] <= j, u, owner)
             base = jnp.where(offs[u] <= j, offs[u], base)
-        block = meta_s[owner, 0, j - base]
+        block = meta_s[owner, 0, jnp.minimum(j - base, MAXB - 1)]
         own_s[j] = owner
         blk_s[j] = block
         grp_s[j] = j if j < NPAIR - 1 else NPAIR - 1 + block
@@ -319,7 +315,7 @@
         tstat[b] = jnp.where(lane_r == 2, peak, jnp.where(lane_r == 3, total, 0.0))
         return carry
 
-    lax.fori_loop(0, NB, teach, 0)
+    lax.fori_loop(0, NB, teach, 0, unroll=True)
     column = lax.broadcasted_iota(jnp.int32, (SUB, VPART), 1).astype(F32)
 
     def leave(j, carry):
@@ -339,7 +335,7 @@
         pst[j] = out
         return carry
 
-    lax.fori_loop(0, NPAIR, leave, 0)
+    lax.fori_loop(0, NPAIR, leave, 0, unroll=4)
     stats = [pst[pl.ds(q * 8, 8)].reshape(LANE, LANE).T[0:8, :] for q in range(2)]
     st_x[px] = jnp.concatenate(stats, axis=1)
     share(st_x, px, x_peers, 2)
@@ -375,7 +371,7 @@
         start = start + jnp.where(u < sec, counts[u], 0)
     for k in range(MAXB):
         row = tot_v[pl.ds(start + k, 1), :]
-        out_ref[0, pl.ds(k, 1), :] = jnp.where(k < ec_s[0], row, 0.0)
+        out_ref[0, pl.ds(k, 1), :] = jnp.where(k < ec_s[0, 0], row, 0.0)
     for copy in sends:
         copy.wait_send()
 
@@ -393,7 +389,7 @@
         out_specs=pl.BlockSpec(memory_space=pltpu.VMEM),
         scratch_shapes=[
             pltpu.SMEM((1, MAXB), i32),
-            pltpu.SMEM((1,), i32),
+            pltpu.SMEM((1, 1), i32),
             pltpu.SMEM((NS, 1, LANE), i32),
             pltpu.SMEM((NPAIR,), i32),
             pltpu.SMEM((NPAIR,), i32),
@@ -401,8 +397,7 @@
             vm((NC, LANE), F32),
             vm((NB, BLK), i32),
             vm((NB, SUB, feat), bf16),
-            vm((1, LANE), i32),
-            vm((NS, 1, LANE), i32),
+            vm((NB, NS, SUB, feat), bf16),
             vm((NC, NS, NB, SUB, LANE), bf16),
             vm((NS, NB, SUB, LANE), F32),
             vm((24, SUB, LANE), F32),
@@ -420,7 +415,7 @@
             vm((TZ, 8, NPAIR * SUB), F32),
             vm((NS, NPAIR, LANE), F32),
             vm((24, LANE), F32),
-            dma((10,)),
+            dma((11,)),
             dma((NT,)),
             dma((NS - 1,)),
             dma((NS,)),
@@ -434,11 +429,11 @@
             dma((NS,)),
         ],
         compiler_params=pltpu.CompilerParams(
-            collective_id=0, has_side_effects=True, vmem_limit_bytes=48 * 1024 * 1024
+            collective_id=0, has_side_effects=True, vmem_limit_bytes=60 * 1024 * 1024
         ),
     )(
         exit_blocks,
-        exit_counts,
+        exit_counts.reshape(1, 1),
         norm_gain.reshape(NC, LANE),
         targets.reshape(NB, BLK),
         stream_in.reshape(NB, NS, SUB, feat),

time: 66.2 us -> 60.1 us (0.908)
  local copies, waits for them, and re-layouts: 4.67 us -> 1.26 us
  Pallas kernels: 60.6 us -> 58.1 us
    unnamed x11 -> x1, local copies, waits for them, and re-layouts: 4.67 us -> 1.26 us
    pallas_call x1, Pallas kernels: 60.6 us -> 58.1 us  [body(): pl.pallas_call(kernel, out_shape=jax.ShapeDtypeStruct((1, MAXB, BLK), F32...]
where the time goes in v2:
time: 60.1 us; the launch traced here: 60 us
  Pallas kernels  58.1 us (97%)
  local copies, waits for them, and re-layouts  1.26 us (2%)
  between operations  0.66 us (1%)
    pallas_call x1, Pallas kernels, body(): pl.pallas_call(kernel, out_shape=jax.ShapeDtypeStruct((1, MAXB, BLK), F32...  58.1 us
    unnamed x1, local copies, waits for them, and re-layouts  1.26 us

profile of v2, /device:TPU:1, one launch (start us, length us, event | category | flops | bytes accessed | tf_op | source)
XLA Modules:
  0.0 60.0 jit_solution(12582410643514644904)
XLA Ops:
  0.7 58.1 %shard_map.73 = f32[1,4,128]{2,1,0:T(4,128)} custom-call(s32[1,4]{1,0:T(1,128)} %eb_hbm.1, s32[1,1]{1,0:T(1,128)} %bitcast.6.ec_hbm, f32[4,128]{1,0:T(4,128)} %bitcast.10, s32[4,128]{1,0:T(4,128)} %bitcast.11, bf16[4,8,16,512]{3,2,1,0:T(8,128)(2,1)} %bitcast.8, bf16[4,8,16,512]{3,2,1,0:T(8,128)(2,1)} %bitcast.9, bf16[16,512,1024]{2,1,0:T(8,128)(2,1)} %bitcast.7), custom_call_target="tpu_custom_call" | custom-call | tf_op jit(solution)/shard_map/pallas_call | solution.py:385
  58.7 1.3 %copy.10 = f32[1,4,128]{2,1,0:T(4,128)} copy(f32[1,4,128]{2,1,0:T(4,128)} %shard_map.73) | data formatting | bytes 4096

commit v3 on v2

--- a/solution.py
+++ b/solution.py
@@ -1,4 +1,5 @@
 import functools
+import heapq
 import itertools
 
 import jax
@@ -29,7 +30,8 @@
 UP = 2.0 ** 58
 F32 = jnp.float32
 MESH = pl.DeviceIdType.MESH
-ORDER = (0, 2, 1, 3)
+ORDER = (0, 2, 3, 1)
+HOP, LAND, GAP, DOT, DEPTH = 1.68, 2.2, 1.3, 0.33, 1
 
 
 def long_sign(c):
@@ -61,56 +63,71 @@
     return v - 4 if v == 3 else v
 
 
-def events():
-    out = []
-    for dist in range(1, 5):
-        for c in ORDER:
-            go = long_sign(c)
-            places = [(2, 0), (-go, 0), (go, 0), (2, -go), (2, go), (-go, -go), (go, -go), (0, -go)]
-            places += [(-go, go), (go, go), (0, go), (0, 2), (-go, 2), (go, 2), (2, 2)]
-            out += [(c, a, b) for a, b in places if abs(a) + abs(b) == dist]
-    return out
+def ahead(c, a, b):
+    return max([1 + ahead(c, *moved(a, b, axis, sign)) for axis, sign in forwards(c, a, b)], default=0)
+
+
+def moved(a, b, axis, sign):
+    return (wrap(a - sign), b) if axis == 0 else (a, wrap(b - sign))
 
 
 def plan():
-    ready = {(0, 0): 2, (0, 1): 2}
-    queue = [(0, 0), (0, 1)]
-    steps = []
-    for c, a, b in events():
-        steps.append(("wait", c, a, b))
+    tick = itertools.count()
+    heap = [(GAP * i, 0, next(tick), ("own", c, 0, 0)) for i, c in enumerate(ORDER)]
+    pending, loaded, free, ready = {}, {}, {}, {}
+    steps, dots = [], []
+
+    def feed(hop, now):
+        queue = pending.get(hop, [])
+        while queue and loaded.get(hop, 0) <= DEPTH:
+            queue.sort()
+            _, _, _, c, a, b, axis, sign = queue.pop(0)
+            free[hop] = max(now, free.get(hop, 0.0)) + HOP
+            loaded[hop] = loaded.get(hop, 0) + 1
+            steps.append(("send", c, a, b, axis, sign))
+            heapq.heappush(heap, (free[hop], 2, next(tick), ("free", hop)))
+            landed = ("wait", c) + moved(a, b, axis, sign)
+            heapq.heappush(heap, (free[hop] + LAND, 1, next(tick), landed))
+
+    now = 0.0
+    while heap:
+        at, _, _, event = heapq.heappop(heap)
+        now = max(now, at)
+        if event[0] == "free":
+            loaded[event[1]] -= 1
+            feed(event[1], at)
+            continue
+        steps.append(event)
+        _, c, a, b = event
+        for axis, sign in forwards(c, a, b):
+            hop = step_of(c, axis, sign)
+            rank = (-ahead(c, *moved(a, b, axis, sign)), ORDER.index(c), next(tick))
+            pending.setdefault(hop, []).append(rank + (c, a, b, axis, sign))
+        for axis, sign in forwards(c, a, b):
+            feed(step_of(c, axis, sign), now)
         key = (rel_of(c, a, b), c // 2)
         ready[key] = ready.get(key, 0) + 1
         if ready[key] == 2:
-            queue.append(key)
-        if queue:
-            steps.append(("dot",) + queue.pop(0))
-    return steps + [("dot",) + key for key in queue]
+            dots.append(("dot",) + key)
+        if dots and event[0] == "wait":
+            steps.append(dots.pop(0))
+            now += DOT
+    return steps + dots
 
 
 STEPS = plan()
 FIRST_USE = list(dict.fromkeys(s[1] for s in STEPS if s[0] == "dot"))
 
 
-def merge(parts):
-    peak_e = functools.reduce(jnp.maximum, [p[0:1] for p in parts])
-    peak_t = functools.reduce(jnp.maximum, [p[2:3] for p in parts])
-    sum_e = sum_t = cross = picked = 0.0
-    for p in parts:
-        fe = jnp.exp(p[0:1] - peak_e)
-        ft = jnp.exp(p[2:3] - peak_t)
-        sum_e = sum_e + p[1:2] * fe
-        sum_t = sum_t + p[3:4] * ft
-        cross = cross + p[4:5] * ft
-        picked = picked + p[5:6]
-    return peak_e, sum_e, peak_t, sum_t, cross, picked
+FAR_FIRST = sorted(range(1, NT), key=lambda k: -abs(wrap(k // TZ)) - abs(wrap(k % TZ)))
 
 
 def kernel(
     eb_hbm, ec_hbm, gain_hbm, tgt_hbm, stream_hbm, delta_hbm, w_hbm, out_ref,
     eb_s, ec_s, meta_s, own_s, blk_s, grp_s,
     gain_v, tgt_v, stream_v, delta_v, abuf, hid, sq, gath, wv, acc,
-    ss_x, ss_z, scale_v, prob_v, tstat, tcol, pst, st_x, st_z, loss_y, tot_v,
-    loc_sem, w_sem, meta_send, meta_recv, a_send, a_recv, g_send, g_recv, ex_send, ex_recv, y_send, y_recv,
+    ss_x, ss_z, scale_v, prob_v, tstat, tcol, pst, stat_v, loss_y, tot_v,
+    loc_sem, w_sem, meta_send, meta_recv, a_send, a_recv, g_send, g_recv, ex_send, ex_recv, st_send, st_recv, y_send, y_recv,
 ):
     sec = lax.axis_index("section")
     tp = lax.axis_index("tp")
@@ -119,9 +136,10 @@
     def plane(dx, dz):
         return (sec, ((px + dx) % TX) * TZ + (pz + dz) % TZ)
 
-    sec_peers = [((sec + k) % NS, tp) for k in range(1, NS)]
+    sec_peers = [((sec + k) % NS, tp) for k in (4, 3, 5, 2, 6, 1, 7)]
     x_peers = [plane(k, 0) for k in range(1, TX)]
     z_peers = [plane(0, k) for k in range(1, TZ)]
+    tp_peers = [plane(k // TZ, k % TZ) for k in FAR_FIRST]
     everyone = sec_peers + x_peers + z_peers
 
     barrier = pltpu.get_barrier_semaphore()
@@ -215,45 +233,32 @@
 
     hop = itertools.count()
 
-    def pass_on(c, a, b):
-        rel = rel_of(c, a, b)
-        for axis, sign in forwards(c, a, b):
-            aa, bb = (wrap(a - sign), b) if axis == 0 else (a, wrap(b - sign))
-            there = rel_of(c, aa, bb)
-            send(
-                gath.at[rel, c], gath.at[there, c],
-                g_send.at[next(hop)], g_recv.at[there, c],
-                plane(*step_of(c, axis, sign)),
-            )
-
-    for n, c in enumerate(ORDER):
+    def pass_on(c, a, b, axis, sign):
+        there = rel_of(c, *moved(a, b, axis, sign))
+        send(
+            gath.at[rel_of(c, a, b), c], gath.at[there, c],
+            g_send.at[next(hop)], g_recv.at[there, c],
+            plane(*step_of(c, axis, sign)),
+        )
+
+    def own_shard(c):
         own_delta[c].wait()
         for peer in sec_peers:
             arrived(abuf.at[c, peer[0]], a_recv.at[c, peer[0]], a_send.at[0, 0])
-        lanes = pl.ds(c * LANE, LANE)
-        state = stream_v[:, :, lanes].astype(F32)
+        state = stream_v[:, :, pl.ds(c * LANE, LANE)].astype(F32)
         for u in range(NS):
             state = state + abuf[c, u].astype(F32)
             hid[u] = state
         gain = gain_v[c : c + 1, :] * DOWN
 
-        def put(g, rows, c=c, n=n, gain=gain):
-            sq[g] = rows * rows if n == 0 else sq[g] + rows * rows
+        def put(g, rows):
+            sq[g] = rows * rows if c == ORDER[0] else sq[g] + rows * rows
             gath[0, c, pl.ds(g * SUB, SUB), :] = (rows * gain).astype(jnp.bfloat16)
 
         for j in range(NPAIR - 1):
             put(j, hid[own_s[j], blk_s[j]])
         for b in range(NB):
             put(NPAIR - 1 + b, hid[NS - 1, b])
-        pass_on(c, 0, 0)
-
-    for g in range(NG, 24):
-        sq[g] = jnp.zeros((SUB, LANE), F32)
-    sums = []
-    for q in range(3):
-        part = sq[pl.ds(q * 8, 8)].reshape(LANE, LANE)
-        sums.append(jnp.sum(part.T, axis=0, keepdims=True))
-    ss_x[px] = jnp.concatenate(sums + [jnp.zeros((5, LANE), F32)], axis=0)
 
     def share(buf, place, peers, stage):
         for k, peer in enumerate(peers):
@@ -264,22 +269,37 @@
             there = (place + k) % 4
             arrived(buf.at[there], ex_recv.at[stage, there], ex_send.at[stage, 0])
 
-    share(ss_x, px, x_peers, 0)
+    def squares():
+        for g in range(NG, 24):
+            sq[g] = jnp.zeros((SUB, LANE), F32)
+        sums = []
+        for q in range(3):
+            part = sq[pl.ds(q * 8, 8)].reshape(LANE, LANE)
+            sums.append(jnp.sum(part.T, axis=0, keepdims=True))
+        ss_x[px] = jnp.concatenate(sums + [jnp.zeros((5, LANE), F32)], axis=0)
+        share(ss_x, px, x_peers, 0)
 
     seen = set()
-    waits = 0
+    waits = owns = 0
     for step in STEPS:
-        if step[0] == "wait":
+        if step[0] == "own":
+            own_shard(step[1])
+            owns += 1
+            first_wait = waits
+        elif step[0] == "send":
+            pass_on(*step[1:])
+        elif step[0] == "wait":
             _, c, a, b = step
             rel = rel_of(c, a, b)
             arrived(gath.at[rel, c], g_recv.at[rel, c], g_send.at[0])
-            pass_on(c, a, b)
             waits += 1
-            if waits == 12:
+            if owns == NC and waits == first_wait + 1:
+                squares()
+            if owns == NC and waits == first_wait + 10:
                 collect(ss_x, px, 0)
                 ss_z[pz] = ss_x[0] + ss_x[1] + ss_x[2] + ss_x[3]
                 share(ss_z, pz, z_peers, 1)
-            if waits == 36:
+            if owns == NC and waits == first_wait + 24:
                 collect(ss_z, pz, 1)
                 total = ss_z[0] + ss_z[1] + ss_z[2] + ss_z[3]
                 scale = lax.rsqrt(total / WIDTH + EPS) * UP
@@ -336,18 +356,33 @@
         return carry
 
     lax.fori_loop(0, NPAIR, leave, 0, unroll=4)
-    stats = [pst[pl.ds(q * 8, 8)].reshape(LANE, LANE).T[0:8, :] for q in range(2)]
-    st_x[px] = jnp.concatenate(stats, axis=1)
-    share(st_x, px, x_peers, 2)
-    collect(st_x, px, 2)
-    joined = merge([st_x[i] for i in range(TX)])
-    st_z[pz] = jnp.concatenate(list(joined) + [jnp.zeros((2, NPAIR * SUB), F32)], axis=0)
-    share(st_z, pz, z_peers, 3)
-    collect(st_z, pz, 3)
-    peak_e, sum_e, peak_t, sum_t, cross, picked = merge([st_z[i] for i in range(TZ)])
-    log_e = jnp.log(sum_e) + peak_e
-    log_t = jnp.log(sum_t) + peak_t
-    loss = 2.0 * log_e - picked + cross / sum_t - log_t
+    halves = []
+    for q in range(2):
+        st = pst[pl.ds(q * 8, 8)].reshape(LANE, LANE).T
+        lse_e = st[0:1, :] + jnp.log(st[1:2, :])
+        lse_t = st[2:3, :] + jnp.log(st[3:4, :])
+        halves += [lse_e, lse_t, st[4:5, :] / st[3:4, :], st[5:6, :]]
+    stat_v[tp] = jnp.concatenate(halves, axis=0)
+    for k, (_, there) in enumerate(tp_peers):
+        send(stat_v.at[tp], stat_v.at[tp], st_send.at[k], st_recv.at[tp], (sec, there))
+    for _, there in tp_peers:
+        arrived(stat_v.at[there], st_recv.at[there], st_send.at[0])
+    parts = [stat_v[i] for i in range(NT)]
+    peak = functools.reduce(jnp.maximum, parts)
+    mass = picked = cross = 0.0
+    for p in parts:
+        share_of = jnp.exp(p - peak)
+        mass = mass + share_of
+        cross = cross + pltpu.roll(share_of, 1, 0) * p
+        picked = picked + p
+    lse = peak + jnp.log(mass)
+    loss = jnp.concatenate(
+        [
+            2.0 * lse[q : q + 1] - picked[q + 3 : q + 4] + cross[q + 2 : q + 3] / mass[q + 1 : q + 2] - lse[q + 1 : q + 2]
+            for q in (0, 4)
+        ],
+        axis=1,
+    )
 
     at = lax.broadcasted_iota(jnp.int32, (NPAIR, NPAIR * SUB), 1) // SUB
     pair = lax.broadcasted_iota(jnp.int32, (NPAIR, NPAIR * SUB), 0)
@@ -356,15 +391,19 @@
     for shift in (64, 32, 16):
         spread = spread + pltpu.roll(spread, shift, 1)
     place = lax.broadcasted_iota(jnp.int32, (NPAIR, LANE), 1) // SUB
-    loss_y[sec] = jnp.where(place == sec, spread, 0.0)
+    low, high = spread[: NPAIR // 2], spread[NPAIR // 2 :]
+    place = place[: NPAIR // 2]
+    loss_y[sec] = jnp.where(place == 0, low, jnp.where(place == 1, high, 0.0))
     for k, peer in enumerate(sec_peers):
         send(loss_y.at[sec], loss_y.at[sec], y_send.at[k], y_recv.at[sec], peer)
     for peer in sec_peers:
         arrived(loss_y.at[peer[0]], y_recv.at[peer[0]], y_send.at[0])
-    total = loss_y[0]
-    for u in range(1, NS):
-        total = total + loss_y[u]
-    tot_v[pl.ds(0, NPAIR)] = total
+    low = high = jnp.zeros((NPAIR // 2, LANE), F32)
+    for u in range(NS):
+        low = jnp.where(place == u, pltpu.roll(loss_y[u], SUB * u, 1), low)
+        high = jnp.where(place == u, pltpu.roll(loss_y[u], (SUB * (u - 1)) % LANE, 1), high)
+    tot_v[pl.ds(0, NPAIR // 2)] = low
+    tot_v[pl.ds(NPAIR // 2, NPAIR // 2)] = high
     tot_v[pl.ds(NPAIR, 8)] = jnp.zeros((8, LANE), F32)
     start = jnp.int32(0)
     for u in range(NS):
@@ -411,9 +450,8 @@
             vm((NB, SUB, LANE), F32),
             vm((NB, SUB, LANE), F32),
             vm((NPAIR, SUB, LANE), F32),
-            vm((TX, 8, NPAIR * SUB), F32),
-            vm((TZ, 8, NPAIR * SUB), F32),
-            vm((NS, NPAIR, LANE), F32),
+            vm((NT, 8, LANE), F32),
+            vm((NS, NPAIR // 2, LANE), F32),
             vm((24, LANE), F32),
             dma((11,)),
             dma((NT,)),
@@ -423,8 +461,10 @@
             dma((NC, NS)),
             dma((NC * (NT - 1),)),
             dma((NT, NC)),
-            dma((4, 3)),
-            dma((4, 4)),
+            dma((2, 3)),
+            dma((2, 4)),
+            dma((NT - 1,)),
+            dma((NT,)),
             dma((NS - 1,)),
             dma((NS,)),
         ],

time: 60.1 us -> 55.5 us (0.923)
  Pallas kernels: 58.1 us -> 53.5 us
    pallas_call x1, Pallas kernels: 58.1 us -> 53.5 us  [body(): pl.pallas_call(kernel, out_shape=jax.ShapeDtypeStruct((1, MAXB, BLK), F32...]
where the time goes in v3:
time: 55.5 us; the launch traced here: 55.4 us
  Pallas kernels  53.5 us (96%)
  local copies, waits for them, and re-layouts  1.26 us (2%)
  between operations  0.66 us (1%)
    pallas_call x1, Pallas kernels, body(): pl.pallas_call(kernel, out_shape=jax.ShapeDtypeStruct((1, MAXB, BLK), F32...  53.5 us
    unnamed x1, local copies, waits for them, and re-layouts  1.26 us

profile of v3, /device:TPU:1, one launch (start us, length us, event | category | flops | bytes accessed | tf_op | source)
XLA Modules:
  0.0 55.4 jit_solution(8856246820015605240)
XLA Ops:
  0.7 53.5 %shard_map.73 = f32[1,4,128]{2,1,0:T(4,128)} custom-call(s32[1,4]{1,0:T(1,128)} %eb_hbm.1, s32[1,1]{1,0:T(1,128)} %bitcast.6.ec_hbm, f32[4,128]{1,0:T(4,128)} %bitcast.10, s32[4,128]{1,0:T(4,128)} %bitcast.11, bf16[4,8,16,512]{3,2,1,0:T(8,128)(2,1)} %bitcast.8, bf16[4,8,16,512]{3,2,1,0:T(8,128)(2,1)} %bitcast.9, bf16[16,512,1024]{2,1,0:T(8,128)(2,1)} %bitcast.7), custom_call_target="tpu_custom_call" | custom-call | tf_op jit(solution)/shard_map/pallas_call | solution.py:424
  54.1 1.3 %copy.10 = f32[1,4,128]{2,1,0:T(4,128)} copy(f32[1,4,128]{2,1,0:T(4,128)} %shard_map.73) | data formatting | bytes 4096

commit v4 on v3

--- a/solution.py
+++ b/solution.py
@@ -140,7 +140,7 @@
     x_peers = [plane(k, 0) for k in range(1, TX)]
     z_peers = [plane(0, k) for k in range(1, TZ)]
     tp_peers = [plane(k // TZ, k % TZ) for k in FAR_FIRST]
-    everyone = sec_peers + x_peers + z_peers
+    everyone = sec_peers + [plane(1, 0), plane(-1, 0), plane(0, 1), plane(0, -1)]
 
     barrier = pltpu.get_barrier_semaphore()
     for peer in everyone:
@@ -355,7 +355,7 @@
         pst[j] = out
         return carry
 
-    lax.fori_loop(0, NPAIR, leave, 0, unroll=4)
+    lax.fori_loop(0, NPAIR, leave, 0, unroll=8)
     halves = []
     for q in range(2):
         st = pst[pl.ds(q * 8, 8)].reshape(LANE, LANE).T
@@ -469,15 +469,15 @@
             dma((NS,)),
         ],
         compiler_params=pltpu.CompilerParams(
-            collective_id=0, has_side_effects=True, vmem_limit_bytes=60 * 1024 * 1024
+            collective_id=0, has_side_effects=True, vmem_limit_bytes=48 * 1024 * 1024
         ),
     )(
-        exit_blocks,
+        pltpu.with_memory_space_constraint(exit_blocks, pltpu.HBM),
         exit_counts.reshape(1, 1),
-        norm_gain.reshape(NC, LANE),
-        targets.reshape(NB, BLK),
-        stream_in.reshape(NB, NS, SUB, feat),
-        layer_delta.reshape(NB, NS, SUB, feat),
+        pltpu.with_memory_space_constraint(norm_gain.reshape(NC, LANE), pltpu.HBM),
+        pltpu.with_memory_space_constraint(targets.reshape(NB, BLK), pltpu.HBM),
+        pltpu.with_memory_space_constraint(stream_in.reshape(NB, NS, SUB, feat), pltpu.HBM),
+        pltpu.with_memory_space_constraint(layer_delta.reshape(NB, NS, SUB, feat), pltpu.HBM),
         out_embed.reshape(NT, NC * LANE, VPART),
     )
 

time: 55.5 us -> 53.8 us (0.969)
  Pallas kernels: 53.5 us -> 52.5 us
  local copies, waits for them, and re-layouts: 1.26 us -> 0.58 us
    pallas_call x1, Pallas kernels: 53.5 us -> 52.5 us  [body(): pl.pallas_call(kernel, out_shape=jax.ShapeDtypeStruct((1, MAXB, BLK), F32...]
    unnamed x1, local copies, waits for them, and re-layouts: 1.26 us -> 0.58 us
where the time goes in v4:
time: 53.8 us; the launch traced here: 53.7 us
  Pallas kernels  52.5 us (98%)
  between operations  0.66 us (1%)
  local copies, waits for them, and re-layouts  0.58 us (1%)
    pallas_call x1, Pallas kernels, body(): pl.pallas_call(kernel, out_shape=jax.ShapeDtypeStruct((1, MAXB, BLK), F32...  52.5 us

profile of v4, /device:TPU:1, one launch (start us, length us, event | category | flops | bytes accessed | tf_op | source)
XLA Modules:
  0.0 53.7 jit_solution(9388093327009577807)
XLA Ops:
  0.7 52.5 %shard_map.73 = f32[1,4,128]{2,1,0:T(4,128)S(1)} custom-call(s32[1,4]{1,0:T(1,128)} %eb_hbm.1, s32[1,1]{1,0:T(1,128)} %bitcast.6.ec_hbm, f32[4,128]{1,0:T(4,128)} %bitcast.10, s32[4,128]{1,0:T(4,128)} %bitcast.11, bf16[4,8,16,512]{3,2,1,0:T(8,128)(2,1)} %bitcast.8, bf16[4,8,16,512]{3,2,1,0:T(8,128)(2,1)} %bitcast.9, bf16[16,512,1024]{2,1,0:T(8,128)(2,1)} %bitcast.7), custom_call_target="tpu_custom_call" | custom-call | tf_op jit(solution)/shard_map/pallas_call | solution.py:424
  53.1 0.6 %copy.10 = f32[1,4,128]{2,1,0:T(4,128)} copy(f32[1,4,128]{2,1,0:T(4,128)S(1)} %shard_map.73) | data formatting | bytes 4096

commit v5 on v4

--- a/solution.py
+++ b/solution.py
@@ -355,7 +355,7 @@
         pst[j] = out
         return carry
 
-    lax.fori_loop(0, NPAIR, leave, 0, unroll=8)
+    lax.fori_loop(0, NPAIR, leave, 0, unroll=True)
     halves = []
     for q in range(2):
         st = pst[pl.ds(q * 8, 8)].reshape(LANE, LANE).T
@@ -363,8 +363,12 @@
         lse_t = st[2:3, :] + jnp.log(st[3:4, :])
         halves += [lse_e, lse_t, st[4:5, :] / st[3:4, :], st[5:6, :]]
     stat_v[tp] = jnp.concatenate(halves, axis=0)
+    early = list(sends)
+    sends.clear()
     for k, (_, there) in enumerate(tp_peers):
         send(stat_v.at[tp], stat_v.at[tp], st_send.at[k], st_recv.at[tp], (sec, there))
+    for copy in early:
+        copy.wait_send()
     for _, there in tp_peers:
         arrived(stat_v.at[there], st_recv.at[there], st_send.at[0])
     parts = [stat_v[i] for i in range(NT)]
@@ -394,8 +398,12 @@
     low, high = spread[: NPAIR // 2], spread[NPAIR // 2 :]
     place = place[: NPAIR // 2]
     loss_y[sec] = jnp.where(place == 0, low, jnp.where(place == 1, high, 0.0))
+    early = list(sends)
+    sends.clear()
     for k, peer in enumerate(sec_peers):
         send(loss_y.at[sec], loss_y.at[sec], y_send.at[k], y_recv.at[sec], peer)
+    for copy in early:
+        copy.wait_send()
     for peer in sec_peers:
         arrived(loss_y.at[peer[0]], y_recv.at[peer[0]], y_send.at[0])
     low = high = jnp.zeros((NPAIR // 2, LANE), F32)

time: 53.8 us -> 53.2 us (0.989)
  Pallas kernels: 52.5 us -> 51.9 us
    pallas_call x1, Pallas kernels: 52.5 us -> 51.9 us  [body(): pl.pallas_call(kernel, out_shape=jax.ShapeDtypeStruct((1, MAXB, BLK), F32...]
where the time goes in v5:
time: 53.2 us; the launch traced here: 53.1 us
  Pallas kernels  51.9 us (98%)
  between operations  0.66 us (1%)
  local copies, waits for them, and re-layouts  0.58 us (1%)
    pallas_call x1, Pallas kernels, body(): pl.pallas_call(kernel, out_shape=jax.ShapeDtypeStruct((1, MAXB, BLK), F32...  51.9 us

profile of v5, /device:TPU:1, one launch (start us, length us, event | category | flops | bytes accessed | tf_op | source)
XLA Modules:
  0.0 53.1 jit_solution(9000508979577981855)
XLA Ops:
  0.7 51.9 %shard_map.73 = f32[1,4,128]{2,1,0:T(4,128)S(1)} custom-call(s32[1,4]{1,0:T(1,128)} %eb_hbm.1, s32[1,1]{1,0:T(1,128)} %bitcast.6.ec_hbm, f32[4,128]{1,0:T(4,128)} %bitcast.10, s32[4,128]{1,0:T(4,128)} %bitcast.11, bf16[4,8,16,512]{3,2,1,0:T(8,128)(2,1)} %bitcast.8, bf16[4,8,16,512]{3,2,1,0:T(8,128)(2,1)} %bitcast.9, bf16[16,512,1024]{2,1,0:T(8,128)(2,1)} %bitcast.7), custom_call_target="tpu_custom_call" | custom-call | tf_op jit(solution)/shard_map/pallas_call | solution.py:432
  52.5 0.6 %copy.10 = f32[1,4,128]{2,1,0:T(4,128)} copy(f32[1,4,128]{2,1,0:T(4,128)S(1)} %shard_map.73) | data formatting | bytes 4096

commit v6 on v5

--- a/solution.py
+++ b/solution.py
@@ -87,7 +87,7 @@
             steps.append(("send", c, a, b, axis, sign))
             heapq.heappush(heap, (free[hop], 2, next(tick), ("free", hop)))
             landed = ("wait", c) + moved(a, b, axis, sign)
-            heapq.heappush(heap, (free[hop] + LAND, 1, next(tick), landed))
+            heapq.heappush(heap, (free[hop] + LAND + 0.01 * ORDER.index(c), 1, next(tick), landed))
 
     now = 0.0
     while heap:
@@ -101,7 +101,7 @@
         _, c, a, b = event
         for axis, sign in forwards(c, a, b):
             hop = step_of(c, axis, sign)
-            rank = (-ahead(c, *moved(a, b, axis, sign)), ORDER.index(c), next(tick))
+            rank = (-ahead(c, *moved(a, b, axis, sign)), -ORDER.index(c), next(tick))
             pending.setdefault(hop, []).append(rank + (c, a, b, axis, sign))
         for axis, sign in forwards(c, a, b):
             feed(step_of(c, axis, sign), now)
@@ -223,13 +223,6 @@
     local[2].wait()
     local[3].wait()
     local[4].wait()
-    lane_r = lax.broadcasted_iota(jnp.int32, (SUB, LANE), 1)
-    sub_r = lax.broadcasted_iota(jnp.int32, (SUB, LANE), 0)
-    mine = lane_r == sec * SUB + sub_r
-    for b in range(NB):
-        row = jnp.broadcast_to(tgt_v[b : b + 1, :].astype(F32), (SUB, LANE))
-        col = jnp.sum(jnp.where(mine, row, 0.0), axis=1, keepdims=True)
-        tcol[b] = jnp.broadcast_to(col, (SUB, LANE)) - (tp * VPART).astype(F32)
 
     hop = itertools.count()
 
@@ -278,6 +271,16 @@
             sums.append(jnp.sum(part.T, axis=0, keepdims=True))
         ss_x[px] = jnp.concatenate(sums + [jnp.zeros((5, LANE), F32)], axis=0)
         share(ss_x, px, x_peers, 0)
+
+    lane_r = lax.broadcasted_iota(jnp.int32, (SUB, LANE), 1)
+
+    def columns():
+        sub_r = lax.broadcasted_iota(jnp.int32, (SUB, LANE), 0)
+        mine = lane_r == sec * SUB + sub_r
+        for b in range(NB):
+            row = jnp.broadcast_to(tgt_v[b : b + 1, :].astype(F32), (SUB, LANE))
+            col = jnp.sum(jnp.where(mine, row, 0.0), axis=1, keepdims=True)
+            tcol[b] = jnp.broadcast_to(col, (SUB, LANE)) - (tp * VPART).astype(F32)
 
     seen = set()
     waits = owns = 0
@@ -295,6 +298,7 @@
             waits += 1
             if owns == NC and waits == first_wait + 1:
                 squares()
+                columns()
             if owns == NC and waits == first_wait + 10:
                 collect(ss_x, px, 0)
                 ss_z[pz] = ss_x[0] + ss_x[1] + ss_x[2] + ss_x[3]

time: 53.2 us -> 53.2 us (level)
  no operation moved by 1% of the time
where the time goes in v6:
time: 53.2 us; the launch traced here: 53.1 us
  Pallas kernels  51.9 us (98%)
  between operations  0.66 us (1%)
  local copies, waits for them, and re-layouts  0.58 us (1%)
    pallas_call x1, Pallas kernels, body(): pl.pallas_call(kernel, out_shape=jax.ShapeDtypeStruct((1, MAXB, BLK), F32...  51.9 us

profile of v6, /device:TPU:1, one launch (start us, length us, event | category | flops | bytes accessed | tf_op | source)
XLA Modules:
  0.0 53.1 jit_solution(18036297688734473941)
XLA Ops:
  0.7 51.9 %shard_map.73 = f32[1,4,128]{2,1,0:T(4,128)S(1)} custom-call(s32[1,4]{1,0:T(1,128)} %eb_hbm.1, s32[1,1]{1,0:T(1,128)} %bitcast.6.ec_hbm, f32[4,128]{1,0:T(4,128)} %bitcast.10, s32[4,128]{1,0:T(4,128)} %bitcast.11, bf16[4,8,16,512]{3,2,1,0:T(8,128)(2,1)} %bitcast.8, bf16[4,8,16,512]{3,2,1,0:T(8,128)(2,1)} %bitcast.9, bf16[16,512,1024]{2,1,0:T(8,128)(2,1)} %bitcast.7), custom_call_target="tpu_custom_call" | custom-call | tf_op jit(solution)/shard_map/pallas_call | solution.py:436
  52.5 0.6 %copy.10 = f32[1,4,128]{2,1,0:T(4,128)} copy(f32[1,4,128]{2,1,0:T(4,128)S(1)} %shard_map.73) | data formatting | bytes 4096

commit v7 on v6

--- a/solution.py
+++ b/solution.py
@@ -281,6 +281,11 @@
             row = jnp.broadcast_to(tgt_v[b : b + 1, :].astype(F32), (SUB, LANE))
             col = jnp.sum(jnp.where(mine, row, 0.0), axis=1, keepdims=True)
             tcol[b] = jnp.broadcast_to(col, (SUB, LANE)) - (tp * VPART).astype(F32)
+
+    start = jnp.int32(0)
+    for u in range(NS):
+        start = start + jnp.where(u < sec, counts[u], 0)
+    tot_v[pl.ds(NPAIR, 8)] = jnp.zeros((8, LANE), F32)
 
     seen = set()
     waits = owns = 0
@@ -416,10 +421,6 @@
         high = jnp.where(place == u, pltpu.roll(loss_y[u], (SUB * (u - 1)) % LANE, 1), high)
     tot_v[pl.ds(0, NPAIR // 2)] = low
     tot_v[pl.ds(NPAIR // 2, NPAIR // 2)] = high
-    tot_v[pl.ds(NPAIR, 8)] = jnp.zeros((8, LANE), F32)
-    start = jnp.int32(0)
-    for u in range(NS):
-        start = start + jnp.where(u < sec, counts[u], 0)
     for k in range(MAXB):
         row = tot_v[pl.ds(start + k, 1), :]
         out_ref[0, pl.ds(k, 1), :] = jnp.where(k < ec_s[0, 0], row, 0.0)

time: 53.2 us -> 53.2 us (level)
  no operation moved by 1% of the time
where the time goes in v7:
time: 53.2 us; the launch traced here: 53.1 us
  Pallas kernels  51.9 us (98%)
  between operations  0.66 us (1%)
  local copies, waits for them, and re-layouts  0.58 us (1%)
    pallas_call x1, Pallas kernels, body(): pl.pallas_call(kernel, out_shape=jax.ShapeDtypeStruct((1, MAXB, BLK), F32...  51.9 us

profile of v7, /device:TPU:1, one launch (start us, length us, event | category | flops | bytes accessed | tf_op | source)
XLA Modules:
  0.0 53.1 jit_solution(9089954232106632596)
XLA Ops:
  0.7 51.9 %shard_map.73 = f32[1,4,128]{2,1,0:T(4,128)S(1)} custom-call(s32[1,4]{1,0:T(1,128)} %eb_hbm.1, s32[1,1]{1,0:T(1,128)} %bitcast.6.ec_hbm, f32[4,128]{1,0:T(4,128)} %bitcast.10, s32[4,128]{1,0:T(4,128)} %bitcast.11, bf16[4,8,16,512]{3,2,1,0:T(8,128)(2,1)} %bitcast.8, bf16[4,8,16,512]{3,2,1,0:T(8,128)(2,1)} %bitcast.9, bf16[16,512,1024]{2,1,0:T(8,128)(2,1)} %bitcast.7), custom_call_target="tpu_custom_call" | custom-call | tf_op jit(solution)/shard_map/pallas_call | solution.py:437
  52.5 0.6 %copy.10 = f32[1,4,128]{2,1,0:T(4,128)} copy(f32[1,4,128]{2,1,0:T(4,128)S(1)} %shard_map.73) | data formatting | bytes 4096
